TPU v7x, 32 devices: a whole 2x2x4 slice. The times are simulated.
32 devices in a mesh: tile: 8 (over y, x, core), depth: 4 (over z).
Axes of the slice: x: 2, y: 2, z: 4, core: 2. Of those that a mesh axis runs over, the one named last changes fastest.
Arguments:
- initial_state: float32 [2, 32, 8192], P(None, 'depth', 'tile'), may hold values from -6 to 6
- observed: float32 [2, 32, 8192], P(None, 'depth', 'tile'), may hold values from -6 to 6
- edge_weight: float32 [8192], P('tile'), may hold values from 0.25 to 1
- land: int32 [8192], P('tile'), may hold values 0 or 1
- w_in: bfloat16 [64, 640], replicated, may hold values from -0.75 to 0.75
- b_in: float32 [640], replicated, may hold values from -3 to 3
- w_mid: bfloat16 [640, 640], replicated, may hold values from -0.25 to 0.25
- b_mid: float32 [640], replicated, may hold values from -3 to 3
- w_out: bfloat16 [640, 64], replicated, may hold values from -0.25 to 0.25
- b_out: float32 [64], replicated, may hold values from -3 to 3
Outputs:
- final_state: float32 [2, 32, 8192], P(None, 'depth', 'tile')
- sensitivity: float32 [2, 32, 8192], P(None, 'depth', 'tile')
- grad_w_in: float32 [64, 640], replicated
- grad_b_in: float32 [640], replicated
- grad_w_mid: float32 [640, 640], replicated
- grad_b_mid: float32 [640], replicated
- grad_w_out: float32 [640, 64], replicated
- grad_b_out: float32 [64], replicated
All inputs are finite; a program needn't handle non-finite values. No bound on the sum of `land` on one device may be relied on, other than what follows from the above.
Results may differ from a plain program's by a relative error of at most 0.0017.
Values may be sent and summed in bfloat16 or wider, within the bound.
No kernel may reach another device: no remote copies, remote signals or barrier semaphores. Data moves between devices by JAX's collectives and lax.ppermute only.
A program may use at most 64 MiB of HBM per device.

v0:
```python
import jax
import jax.numpy as jnp
from jax import lax
from jax.sharding import PartitionSpec as P

TILE_SIDE = 32
LEVELS = 32
TIME_STEPS = 2
FEATURES = 64
TILE_CELLS = 1024
diffuse_coef = 0.2
step_size = 0.5


def with_halo(cells, sides, width):
    for axis, dim in sides:
        count = lax.axis_size(axis)
        head = lax.slice_in_dim(cells, 0, width, axis=dim)
        tail = lax.slice_in_dim(cells, cells.shape[dim] - width, cells.shape[dim], axis=dim)
        cells = jnp.concatenate(
            [
                lax.ppermute(tail, axis, [(i, (i + 1) % count) for i in range(count)]),
                cells,
                lax.ppermute(head, axis, [((i + 1) % count, i) for i in range(count)]),
            ],
            axis=dim,
        )
    return cells


def passed_along(x, axis, by):
    length = lax.axis_size(axis)
    return lax.ppermute(x, axis, [(i, (i + by) % length) for i in range(length)])


def neighbour_sum(flat_rows):
    row_count = flat_rows.shape[0]
    tile_grid = flat_rows.reshape(row_count, TILE_SIDE, TILE_SIDE)
    zonal_pair = jnp.stack([tile_grid[:, :, -1], tile_grid[:, :, 0]], axis=1)
    padded = with_halo(zonal_pair[None], (("tile", 0),), 1)
    from_west = padded[0, :, 0, :]
    from_east = padded[2, :, 1, :]
    fold_pair = jnp.stack([tile_grid[:, 0, :], tile_grid[:, -1, :]], axis=1)
    across = passed_along(fold_pair, "tile", lax.axis_size("tile") // 2)[:, :, ::-1]
    west_cells = jnp.concatenate([from_west[:, :, None], tile_grid[:, :, :-1]], axis=2)
    east_cells = jnp.concatenate([tile_grid[:, :, 1:], from_east[:, :, None]], axis=2)
    south_cells = jnp.concatenate([across[:, 0, None, :], tile_grid[:, :-1, :]], axis=1)
    north_cells = jnp.concatenate([tile_grid[:, 1:, :], across[:, 1, None, :]], axis=1)
    return (west_cells + east_cells + south_cells + north_cells).reshape(row_count, TILE_CELLS)


def diffuse(tracer_field, weight, weight_sums):
    flat_rows = tracer_field.reshape(-1, TILE_CELLS)
    scaled = flat_rows * weight[None, :]
    result_rows = weight[None, :] * (neighbour_sum(scaled) - flat_rows * weight_sums[None, :])
    return result_rows.reshape(tracer_field.shape)


def silu_slope(pre_act):
    sigmoid_val = jax.nn.sigmoid(pre_act)
    return sigmoid_val * (1.0 + pre_act * (1.0 - sigmoid_val))


def closure_forward(inputs, params):
    w_in, b_in, w_mid, b_mid, w_out, b_out = params
    contract_rows = (((0,), (0,)), ((), ()))
    pre_one = (
        lax.dot_general(w_in, inputs, contract_rows, preferred_element_type=jnp.float32)
        + b_in[:, None]
    )
    hidden_one = jax.nn.silu(pre_one).astype(jnp.bfloat16)
    pre_two = (
        lax.dot_general(w_mid, hidden_one, contract_rows, preferred_element_type=jnp.float32)
        + b_mid[:, None]
    )
    hidden_two = jax.nn.silu(pre_two).astype(jnp.bfloat16)
    output = (
        lax.dot_general(w_out, hidden_two, contract_rows, preferred_element_type=jnp.float32)
        + b_out[:, None]
    )
    return (output, (inputs, pre_one, hidden_one, pre_two, hidden_two))


def closure_backward(upstream, saved_cache, params):
    w_in, b_in, w_mid, b_mid, w_out, b_out = params
    inputs, pre_one, hidden_one, pre_two, hidden_two = saved_cache
    contract_cols = (((1,), (1,)), ((), ()))
    grad_w_out = lax.dot_general(
        hidden_two, upstream, contract_cols, preferred_element_type=jnp.float32
    )
    grad_b_out = jnp.sum(upstream.astype(jnp.float32), axis=1)
    slope_two = (
        jnp.dot(w_out, upstream, preferred_element_type=jnp.float32) * silu_slope(pre_two)
    ).astype(jnp.bfloat16)
    grad_w_mid = lax.dot_general(
        hidden_one, slope_two, contract_cols, preferred_element_type=jnp.float32
    )
    grad_b_mid = jnp.sum(slope_two.astype(jnp.float32), axis=1)
    slope_one = (
        jnp.dot(w_mid, slope_two, preferred_element_type=jnp.float32) * silu_slope(pre_one)
    ).astype(jnp.bfloat16)
    grad_w_in = lax.dot_general(
        inputs, slope_one, contract_cols, preferred_element_type=jnp.float32
    )
    grad_b_in = jnp.sum(slope_one.astype(jnp.float32), axis=1)
    back_grad = jnp.dot(w_in, slope_one, preferred_element_type=jnp.float32)
    return (back_grad, (grad_w_in, grad_b_in, grad_w_mid, grad_b_mid, grad_w_out, grad_b_out))


def body(initial_state, observed, edge_weight, land, w_in, b_in, w_mid, b_mid, w_out, b_out):
    params = (w_in, b_in, w_mid, b_mid, w_out, b_out)
    ocean_mask = land.astype(jnp.float32)
    weight = edge_weight * ocean_mask
    weight_sums = neighbour_sum(weight[None, :])[0]

    def to_columns(segment):
        full_cols = lax.all_to_all(segment, "depth", split_axis=2, concat_axis=1, tiled=True)
        return full_cols.reshape(FEATURES, full_cols.shape[2])

    def to_segments(values):
        shaped = values.reshape(2, LEVELS, values.shape[1])
        segment_part = lax.all_to_all(shaped, "depth", split_axis=1, concat_axis=2, tiled=True)
        return segment_part

    state_now = initial_state
    caches = []
    for step_index in range(TIME_STEPS):
        inputs = to_columns(state_now.astype(jnp.bfloat16))
        tendency, saved_cache = closure_forward(inputs, params)
        caches.append(saved_cache)
        change = diffuse(state_now, weight, weight_sums)
        state_now = (
            state_now
            + diffuse_coef * change
            + step_size * ocean_mask[None, None, :] * to_segments(tendency)
        )
    adjoint = ocean_mask[None, None, :] * (state_now - observed)
    grad_list = []
    for step_index in reversed(range(TIME_STEPS)):
        upstream = to_columns(
            (step_size * ocean_mask[None, None, :] * adjoint).astype(jnp.bfloat16)
        )
        back_grad, param_grads = closure_backward(upstream, caches[step_index], params)
        grad_list.append(param_grads)
        spread = diffuse(adjoint, weight, weight_sums)
        adjoint = adjoint + diffuse_coef * spread + to_segments(back_grad)
    totals = grad_list[0]
    for param_grads in grad_list[1:]:
        totals = tuple((total + gradient for total, gradient in zip(totals, param_grads)))
    summed = lax.psum(totals, ("tile", "depth"))
    grad_scale = 1.0 / (lax.axis_size("tile") * TILE_CELLS)
    return (
        state_now,
        adjoint,
        summed[0] * grad_scale,
        summed[1] * grad_scale,
        summed[2] * grad_scale,
        summed[3] * grad_scale,
        summed[4] * grad_scale,
        summed[5] * grad_scale,
    )


def solution(mesh):
    return jax.shard_map(
        body,
        mesh=mesh,
        in_specs=(
            P(None, "depth", "tile"),
            P(None, "depth", "tile"),
            P("tile"),
            P("tile"),
            P(),
            P(),
            P(),
            P(),
            P(),
            P(),
        ),
        out_specs=(
            P(None, "depth", "tile"),
            P(None, "depth", "tile"),
            P(),
            P(),
            P(),
            P(),
            P(),
            P(),
        ),
        check_vma=False,
    )
```

profile of v0, /device:TPU:0, one launch (start us, length us, event | category | flops | bytes accessed | tf_op | source)
XLA Modules:
  0.0 276.7 jit_solution(8364587519596231876)
XLA Ops:
  7.2 0.8 convert_multiply_fusion
  8.2 3.4 %collective-permute-start.4 = (f32[1,1,2,32]{3,2,1,0:T(2,128)S(1)}, f32[1,1,2,32]{3,2,1,0:T(2,128)S(1)}, u32[]{:S(2)}, u32[]{:S(2)}) collective-permute-start(f32[1,1,2,32]{3,2,1,0:T(2,128)S(1)} %maximum_bitcast_fusion.4), channel_id=1, source_target_pairs={{4,0},{8,4},{12,8},{16,12},{20,16},{24,20},{28,24},{0,28},{5,1},{9... | collective-permute-start | bytes 776 | tf_op jit(solution)/shard_map/ppermute | solution.py:24
  11.7 1.0 reshape.230
  13.0 2.7 collective-permute-start.1
  16.3 0.8 convert_element_type.60
  17.5 1.1 reshape.252
  18.7 4.9 %all-to-all-start = ((bf16[4,2,2048]{2,1,0:T(2,128)(2,1)}), bf16[4,2,2048]{2,1,0:T(2,128)(2,1)S(1)}, u32[]{:S(2)}, u32[]{:S(2)}) async-start(bf16[4,2,2048]{2,1,0:T(2,128)(2,1)} %reshape.252), calls=%async_computation | async-start | bytes 65536 | tf_op jit(solution)/shard_map/all_to_all | solution.py:117
  23.8 0.7 fusion.33
  25.2 1.5 collective-permute-start.2
  27.2 1.7 collective-permute-done.2
  29.0 0.7 slice.223
  29.7 0.7 slice.219
  32.7 1.3 multiply_convert_fusion.2
  35.0 5.1 %all-to-all-start.1 = ((f32[2,32,256]{2,0,1:T(2,128)}), f32[2,32,256]{2,0,1:T(2,128)}, u32[]{:S(2)}, u32[]{:S(2)}) async-start(f32[2,32,256]{2,0,1:T(2,128)} %copy.161), calls=%async_computation.1 | async-start | bytes 131072 | tf_op jit(solution)/shard_map/all_to_all | solution.py:122
  40.0 1.2 fusion.13
  41.3 4.5 %all-to-all-done.1 = f32[2,32,256]{2,0,1:T(2,128)} async-done(((f32[2,32,256]{2,0,1:T(2,128)}), f32[2,32,256]{2,0,1:T(2,128)}, u32[]{:S(2)}, u32[]{:S(2)}) %all-to-all-start.1) | async-done | bytes 65568 | tf_op jit(solution)/shard_map/all_to_all | solution.py:122
  45.9 0.8 copy.162
  47.9 0.8 fusion.32
  48.7 1.6 collective-permute-start.8
  50.3 0.8 fusion.30
  51.5 1.1 reshape.254
  52.6 3.3 %all-to-all-start.2 = ((bf16[4,2,2048]{2,1,0:T(2,128)(2,1)}), bf16[4,2,2048]{2,1,0:T(2,128)(2,1)S(1)}, u32[]{:S(2)}, u32[]{:S(2)}) async-start(bf16[4,2,2048]{2,1,0:T(2,128)(2,1)} %reshape.254), calls=%async_computation.2 | async-start | bytes 65536 | tf_op jit(solution)/shard_map/all_to_all | solution.py:117
  55.9 0.7 slice.251
  56.7 0.7 slice.247
  57.7 3.8 %all-to-all-done.2 = bf16[4,2,2048]{2,1,0:T(2,128)(2,1)S(1)} async-done(((bf16[4,2,2048]{2,1,0:T(2,128)(2,1)}), bf16[4,2,2048]{2,1,0:T(2,128)(2,1)S(1)}, u32[]{:S(2)}, u32[]{:S(2)}) %all-to-all-start.2) | async-done | bytes 32800 | tf_op jit(solution)/shard_map/all_to_all | solution.py:117
  63.4 2.3 multiply_convert_fusion
  66.6 3.9 %all-to-all-start.3 = ((f32[2,32,256]{2,0,1:T(2,128)}), f32[2,32,256]{2,0,1:T(2,128)}, u32[]{:S(2)}, u32[]{:S(2)}) async-start(f32[2,32,256]{2,0,1:T(2,128)} %copy.168), calls=%async_computation.3 | async-start | bytes 131072 | tf_op jit(solution)/shard_map/all_to_all | solution.py:122
  70.5 1.3 fusion.15
  72.0 4.4 %all-to-all-done.3 = f32[2,32,256]{2,0,1:T(2,128)} async-done(((f32[2,32,256]{2,0,1:T(2,128)}), f32[2,32,256]{2,0,1:T(2,128)}, u32[]{:S(2)}, u32[]{:S(2)}) %all-to-all-start.3) | async-done | bytes 65568 | tf_op jit(solution)/shard_map/all_to_all | solution.py:122
  76.3 0.8 copy.169
  77.2 1.5 multiply_convert_fusion.5
  80.5 0.8 fusion.27
  81.8 1.1 reshape.256
  82.9 4.0 %all-to-all-start.4 = ((bf16[4,2,2048]{2,1,0:T(2,128)(2,1)}), bf16[4,2,2048]{2,1,0:T(2,128)(2,1)}, u32[]{:S(2)}, u32[]{:S(2)}) async-start(bf16[4,2,2048]{2,1,0:T(2,128)(2,1)} %reshape.256), calls=%async_computation.4 | async-start | bytes 65536 | tf_op jit(solution)/shard_map/all_to_all | solution.py:117
  87.0 0.7 slice.265
  88.8 1.3 fusion.17
  90.2 2.3 all-to-all-done.4
  92.5 1.4 reshape.257
  94.2 0.9 fusion.47
  95.1 1.5 convert_reduce_fusion.1
  96.6 1.1 convert_reduce_fusion.3
  97.7 1.7 fusion.22
  99.6 0.7 copy.175
  100.3 3.3 %all-to-all-start.5 = ((f32[2,32,256]{2,0,1:T(2,128)}), f32[2,32,256]{2,0,1:T(2,128)S(1)}, u32[]{:S(2)}, u32[]{:S(2)}) async-start(f32[2,32,256]{2,0,1:T(2,128)} %copy.175), calls=%async_computation.5 | async-start | bytes 131072 | tf_op jit(solution)/shard_map/all_to_all | solution.py:122
  103.6 0.9 fusion.46
  104.5 4.8 %all-to-all-done.5 = f32[2,32,256]{2,0,1:T(2,128)S(1)} async-done(((f32[2,32,256]{2,0,1:T(2,128)}), f32[2,32,256]{2,0,1:T(2,128)S(1)}, u32[]{:S(2)}, u32[]{:S(2)}) %all-to-all-start.5) | async-done | bytes 65568 | tf_op jit(solution)/shard_map/all_to_all | solution.py:122
  110.6 1.6 collective-permute-start.14
  112.2 0.7 fusion.24
  113.3 1.1 reshape.258
  114.4 3.9 %all-to-all-start.6 = ((bf16[4,2,2048]{2,1,0:T(2,128)(2,1)}), bf16[4,2,2048]{2,1,0:T(2,128)(2,1)}, u32[]{:S(2)}, u32[]{:S(2)}) async-start(bf16[4,2,2048]{2,1,0:T(2,128)(2,1)} %reshape.258), calls=%async_computation.6 | async-start | bytes 65536 | tf_op jit(solution)/shard_map/all_to_all | solution.py:117
  119.0 1.2 fusion.19
  120.3 3.7 %all-to-all-done.6 = bf16[4,2,2048]{2,1,0:T(2,128)(2,1)} async-done(((bf16[4,2,2048]{2,1,0:T(2,128)(2,1)}), bf16[4,2,2048]{2,1,0:T(2,128)(2,1)}, u32[]{:S(2)}, u32[]{:S(2)}) %all-to-all-start.6) | async-done | bytes 32800 | tf_op jit(solution)/shard_map/all_to_all | solution.py:117
  124.0 1.4 reshape.259
  125.8 1.8 convolution_add_fusion.5
  127.6 1.5 convert_reduce_fusion
  130.0 0.9 fusion.11
  130.8 1.7 convolution_add_fusion
  132.5 0.7 copy-done.18
  134.3 3.3 %all-to-all-start.7 = ((f32[2,32,256]{2,0,1:T(2,128)}), f32[2,32,256]{2,0,1:T(2,128)S(1)}, u32[]{:S(2)}, u32[]{:S(2)}) async-start(f32[2,32,256]{2,0,1:T(2,128)} %copy.182), calls=%async_computation.7 | async-start | bytes 131072 | tf_op jit(solution)/shard_map/all_to_all | solution.py:122
  137.6 40.0 %all-reduce = (f32[640]{0:T(1024)S(1)}, f32[640]{0:T(1024)S(1)}, f32[64]{0:T(128)S(1)}) all-reduce(f32[640]{0:T(1024)S(1)} %add.309, f32[640]{0:T(1024)S(1)} %add.311, f32[64]{0:T(128)S(1)} %add.314), channel_id=1, replica_groups=mesh['tile'=8,'depth'=4] {'tile','depth'}, use_global_device_ids=true, to_apply=%region_3.4 | all-reduce | flops 1344 | bytes 10752 | tf_op jit(solution)/shard_map/psum | solution.py:150
  180.0 84.0 %all-reduce.4.cloned.1.call-done = (f32[64,640]{1,0:T(8,128)}, f32[640,640]{1,0:T(8,128)}, f32[640,64]{0,1:T(8,128)}) async-done(((f32[64,640]{1,0:T(8,128)}, f32[640,640]{1,0:T(8,128)}, f32[640,64]{0,1:T(8,128)}), (f32[64,640]{1,0:T(8,128)}, f32[640,640]{1,0:T(8,128)}, f32[640,64]{0,1:T(8,128)})) %all-reduce.4.cloned.1.call-update) | async-done | bytes 1966096 | tf_op jit(solution)/shard_map/psum | solution.py:150
  264.0 1.6 broadcast_multiply_fusion.6
  265.6 1.6 broadcast_multiply_fusion.5
  267.2 2.7 broadcast_multiply_fusion
  (192 shorter events, 22.1 us)
Async XLA Ops:
  7.2 25.5 %copy-start = (bf16[640,640]{1,0:T(8,128)(2,1)S(1)}, bf16[640,640]{1,0:T(8,128)(2,1)}, u32[]{:S(2)}) copy-start(bf16[640,640]{1,0:T(8,128)(2,1)} %param.16) | copy-start | bytes 2457604
  8.2 18.7 %collective-permute-start.4 = (f32[1,1,2,32]{3,2,1,0:T(2,128)S(1)}, f32[1,1,2,32]{3,2,1,0:T(2,128)S(1)}, u32[]{:S(2)}, u32[]{:S(2)}) collective-permute-start(f32[1,1,2,32]{3,2,1,0:T(2,128)S(1)} %maximum_bitcast_fusion.4), channel_id=1, source_target_pairs={{4,0},{8,4},{12,8},{16,12},{20,16},{24,20},{28,24},{0,28},{5,1},{9... | collective-permute-start | bytes 776 | tf_op jit(solution)/shard_map/ppermute | solution.py:24
  11.6 13.5 %collective-permute-start.3 = (f32[1,1,2,32]{3,2,1,0:T(2,128)S(1)}, f32[1,1,2,32]{3,2,1,0:T(2,128)S(1)}, u32[]{:S(2)}, u32[]{:S(2)}) collective-permute-start(f32[1,1,2,32]{3,2,1,0:T(2,128)S(1)} %maximum_bitcast_fusion.4), channel_id=1, source_target_pairs={{0,4},{4,8},{8,12},{12,16},{16,20},{20,24},{24,28},{28,0},{1,5},{5... | collective-permute-start | bytes 776 | tf_op jit(solution)/shard_map/ppermute | solution.py:22
  13.0 15.9 %collective-permute-start.1 = (f32[1,16,2,32]{3,1,2,0:T(8,128)S(1)}, f32[1,16,2,32]{3,1,2,0:T(8,128)S(1)}, u32[]{:S(2)}, u32[]{:S(2)}) collective-permute-start(f32[1,16,2,32]{3,1,2,0:T(8,128)S(1)} %maximum_bitcast_fusion), channel_id=1, source_target_pairs={{4,0},{8,4},{12,8},{16,12},{20,16},{24,20},{28,24},{0,28},{5,1},{9... | collective-permute-start | bytes 12296 | tf_op jit(solution)/shard_map/ppermute | solution.py:24
  15.7 13.2 %collective-permute-start = (f32[1,16,2,32]{3,1,2,0:T(8,128)S(1)}, f32[1,16,2,32]{3,1,2,0:T(8,128)S(1)}, u32[]{:S(2)}, u32[]{:S(2)}) collective-permute-start(f32[1,16,2,32]{3,1,2,0:T(8,128)S(1)} %maximum_bitcast_fusion), channel_id=1, source_target_pairs={{0,4},{4,8},{8,12},{12,16},{16,20},{20,24},{24,28},{28,0},{1,5},{5... | collective-permute-start | bytes 12296 | tf_op jit(solution)/shard_map/ppermute | solution.py:22
  15.7 10.9 %collective-permute-start.5 = (f32[1,2,32]{2,1,0:T(2,128)S(1)}, f32[1,2,32]{2,1,0:T(2,128)S(1)}, u32[]{:S(2)}, u32[]{:S(2)}) collective-permute-start(f32[1,2,32]{2,1,0:T(2,128)S(1)} %pad_maximum_fusion.4), channel_id=1, source_target_pairs={{0,16},{4,20},{8,24},{12,28},{16,0},{20,4},{24,8},{28,12},{1,17},{... | collective-permute-start | bytes 776 | tf_op jit(solution)/shard_map/ppermute | solution.py:33
  17.2 7.4 %copy-start.23 = (s32[1024]{0:T(1024)S(1)}, s32[1024]{0:T(1024)}, u32[]{:S(2)}) copy-start(s32[1024]{0:T(1024)} %param.13) | copy-start | bytes 12292
  18.7 12.1 %all-to-all-start = ((bf16[4,2,2048]{2,1,0:T(2,128)(2,1)}), bf16[4,2,2048]{2,1,0:T(2,128)(2,1)S(1)}, u32[]{:S(2)}, u32[]{:S(2)}) async-start(bf16[4,2,2048]{2,1,0:T(2,128)(2,1)} %reshape.252), calls=%async_computation | async-start | bytes 65536 | tf_op jit(solution)/shard_map/all_to_all | solution.py:117
  23.8 8.6 %copy-start.2 = (bf16[64,640]{1,0:T(8,128)(2,1)S(1)}, bf16[64,640]{1,0:T(8,128)(2,1)}, u32[]{:S(2)}) copy-start(bf16[64,640]{1,0:T(8,128)(2,1)} %param.14) | copy-start | bytes 245764
  23.8 8.6 %copy-start.21 = (f32[640]{0:T(1024)S(1)}, f32[640]{0:T(1024)}, u32[]{:S(2)}) copy-start(f32[640]{0:T(1024)} %param.15) | copy-start | bytes 7684
  24.5 8.1 %copy-start.27 = (f32[640]{0:T(1024)S(1)}, f32[640]{0:T(1024)}, u32[]{:S(2)}) copy-start(f32[640]{0:T(1024)} %param.17) | copy-start | bytes 7684
  25.2 3.7 %collective-permute-start.2 = (f32[16,2,32]{2,1,0:T(2,128)S(1)}, f32[16,2,32]{2,1,0:T(2,128)S(1)}, u32[]{:S(2)}, u32[]{:S(2)}) collective-permute-start(f32[16,2,32]{2,1,0:T(2,128)S(1)} %pad_maximum_fusion), channel_id=1, source_target_pairs={{0,16},{4,20},{8,24},{12,28},{16,0},{20,4},{24,8},{28,12},{1,17},{... | collective-permute-start | bytes 12296 | tf_op jit(solution)/shard_map/ppermute | solution.py:33
  31.7 0.6 copy-start.19
  32.7 1.4 copy-start.11
  32.7 1.4 copy-start.25
  34.0 12.7 %copy-start.10 = (f32[2,8,1024]{2,1,0:T(8,128)S(1)}, f32[2,8,1024]{2,1,0:T(8,128)}, u32[]{:S(2)}) copy-start(f32[2,8,1024]{2,1,0:T(8,128)} %param.10) | copy-start | bytes 196612
  35.0 10.9 %all-to-all-start.1 = ((f32[2,32,256]{2,0,1:T(2,128)}), f32[2,32,256]{2,0,1:T(2,128)}, u32[]{:S(2)}, u32[]{:S(2)}) async-start(f32[2,32,256]{2,0,1:T(2,128)} %copy.161), calls=%async_computation.1 | async-start | bytes 131072 | tf_op jit(solution)/shard_map/all_to_all | solution.py:122
  46.8 4.3 %copy-start.9 = (f32[2,8,1024]{2,1,0:T(8,128)}, f32[2,8,1024]{2,1,0:T(8,128)S(1)}, u32[]{:S(2)}) copy-start(f32[2,8,1024]{2,1,0:T(8,128)S(1)} %get-tuple-element.30) | copy-start | bytes 196612
  47.3 8.6 %collective-permute-start.7 = (f32[1,16,2,32]{3,1,2,0:T(8,128)S(1)}, f32[1,16,2,32]{3,1,2,0:T(8,128)S(1)}, u32[]{:S(2)}, u32[]{:S(2)}) collective-permute-start(f32[1,16,2,32]{3,1,2,0:T(8,128)S(1)} %maximum_bitcast_fusion.1), channel_id=1, source_target_pairs={{4,0},{8,4},{12,8},{16,12},{20,16},{24,20},{28,24},{0,28},{5,1},{9... | collective-permute-start | bytes 12296 | tf_op jit(solution)/shard_map/ppermute | solution.py:24
  47.4 8.6 %collective-permute-start.6 = (f32[1,16,2,32]{3,1,2,0:T(8,128)S(1)}, f32[1,16,2,32]{3,1,2,0:T(8,128)S(1)}, u32[]{:S(2)}, u32[]{:S(2)}) collective-permute-start(f32[1,16,2,32]{3,1,2,0:T(8,128)S(1)} %maximum_bitcast_fusion.1), channel_id=1, source_target_pairs={{0,4},{4,8},{8,12},{12,16},{16,20},{20,24},{24,28},{28,0},{1,5},{5... | collective-permute-start | bytes 12296 | tf_op jit(solution)/shard_map/ppermute | solution.py:22
  48.7 7.2 %collective-permute-start.8 = (f32[16,2,32]{2,1,0:T(2,128)S(1)}, f32[16,2,32]{2,1,0:T(2,128)S(1)}, u32[]{:S(2)}, u32[]{:S(2)}) collective-permute-start(f32[16,2,32]{2,1,0:T(2,128)S(1)} %pad_maximum_fusion.1), channel_id=1, source_target_pairs={{0,16},{4,20},{8,24},{12,28},{16,0},{20,4},{24,8},{28,12},{1,17},{... | collective-permute-start | bytes 12296 | tf_op jit(solution)/shard_map/ppermute | solution.py:33
  52.6 8.9 %all-to-all-start.2 = ((bf16[4,2,2048]{2,1,0:T(2,128)(2,1)}), bf16[4,2,2048]{2,1,0:T(2,128)(2,1)S(1)}, u32[]{:S(2)}, u32[]{:S(2)}) async-start(bf16[4,2,2048]{2,1,0:T(2,128)(2,1)} %reshape.254), calls=%async_computation.2 | async-start | bytes 65536 | tf_op jit(solution)/shard_map/all_to_all | solution.py:117
  62.5 0.6 copy-start.15
  63.4 2.3 copy-start.4
  63.4 2.3 copy-start.12
  63.4 2.3 copy-start.26
  63.4 7.1 %copy-start.3 = (f32[16,32,31]{2,1,0:T(8,128)S(1)}, f32[16,32,31]{2,1,0:T(8,128)}, u32[]{:S(2)}) copy-start(f32[16,32,31]{2,1,0:T(8,128)} %get-tuple-element.48) | copy-start | bytes 190468
  65.7 11.5 %copy-start.22 = (f32[1024]{0:T(1024)S(1)}, f32[1024]{0:T(1024)}, u32[]{:S(2)}) copy-start(f32[1024]{0:T(1024)} %convert_element_type.59) | copy-start | bytes 12292
  66.6 9.7 %all-to-all-start.3 = ((f32[2,32,256]{2,0,1:T(2,128)}), f32[2,32,256]{2,0,1:T(2,128)}, u32[]{:S(2)}, u32[]{:S(2)}) async-start(f32[2,32,256]{2,0,1:T(2,128)} %copy.168), calls=%async_computation.3 | async-start | bytes 131072 | tf_op jit(solution)/shard_map/all_to_all | solution.py:122
  78.7 0.6 copy-start.7
  79.2 9.4 %collective-permute-start.10 = (f32[1,16,2,32]{3,1,2,0:T(8,128)S(1)}, f32[1,16,2,32]{3,1,2,0:T(8,128)S(1)}, u32[]{:S(2)}, u32[]{:S(2)}) collective-permute-start(f32[1,16,2,32]{3,1,2,0:T(8,128)S(1)} %maximum_bitcast_fusion.2), channel_id=1, source_target_pairs={{4,0},{8,4},{12,8},{16,12},{20,16},{24,20},{28,24},{0,28},{5,1},{9... | collective-permute-start | bytes 12296 | tf_op jit(solution)/shard_map/ppermute | solution.py:24
  79.3 7.6 %collective-permute-start.9 = (f32[1,16,2,32]{3,1,2,0:T(8,128)S(1)}, f32[1,16,2,32]{3,1,2,0:T(8,128)S(1)}, u32[]{:S(2)}, u32[]{:S(2)}) collective-permute-start(f32[1,16,2,32]{3,1,2,0:T(8,128)S(1)} %maximum_bitcast_fusion.2), channel_id=1, source_target_pairs={{0,4},{4,8},{8,12},{12,16},{16,20},{20,24},{24,28},{28,0},{1,5},{5... | collective-permute-start | bytes 12296 | tf_op jit(solution)/shard_map/ppermute | solution.py:22
  80.0 7.0 %collective-permute-start.11 = (f32[16,2,32]{2,1,0:T(2,128)S(1)}, f32[16,2,32]{2,1,0:T(2,128)S(1)}, u32[]{:S(2)}, u32[]{:S(2)}) collective-permute-start(f32[16,2,32]{2,1,0:T(2,128)S(1)} %pad_maximum_fusion.2), channel_id=1, source_target_pairs={{0,16},{4,20},{8,24},{12,28},{16,0},{20,4},{24,8},{28,12},{1,17},{... | collective-permute-start | bytes 12296 | tf_op jit(solution)/shard_map/ppermute | solution.py:33
  82.9 9.6 %all-to-all-start.4 = ((bf16[4,2,2048]{2,1,0:T(2,128)(2,1)}), bf16[4,2,2048]{2,1,0:T(2,128)(2,1)}, u32[]{:S(2)}, u32[]{:S(2)}) async-start(bf16[4,2,2048]{2,1,0:T(2,128)(2,1)} %reshape.256), calls=%async_computation.4 | async-start | bytes 65536 | tf_op jit(solution)/shard_map/all_to_all | solution.py:117
  90.0 5.0 %copy-start.13 = (bf16[640,64]{0,1:T(8,128)(2,1)S(1)}, bf16[640,64]{0,1:T(8,128)(2,1)}, u32[]{:S(2)}) copy-start(bf16[640,64]{0,1:T(8,128)(2,1)} %param.18) | copy-start | bytes 245764
  94.2 2.4 copy-start.17
  95.1 1.6 copy-start.5
  97.7 5.9 %copy-start.16 = (bf16[2,4,8,256]{3,2,1,0:T(8,128)(2,1)S(1)}, bf16[2,4,8,256]{3,2,1,0:T(8,128)(2,1)}, u32[]{:S(2)}) copy-start(bf16[2,4,8,256]{3,2,1,0:T(8,128)(2,1)} %copy-done.15) | copy-start | bytes 98308
  97.7 11.6 %copy-start.8 = (f32[2,8,1024]{2,1,0:T(8,128)S(1)}, f32[2,8,1024]{2,1,0:T(8,128)}, u32[]{:S(2)}) copy-start(f32[2,8,1024]{2,1,0:T(8,128)} %copy-done.7) | copy-start | bytes 196612
  100.3 9.0 %all-to-all-start.5 = ((f32[2,32,256]{2,0,1:T(2,128)}), f32[2,32,256]{2,0,1:T(2,128)S(1)}, u32[]{:S(2)}, u32[]{:S(2)}) async-start(f32[2,32,256]{2,0,1:T(2,128)} %copy.175), calls=%async_computation.5 | async-start | bytes 131072 | tf_op jit(solution)/shard_map/all_to_all | solution.py:122
  109.9 8.9 %collective-permute-start.13 = (f32[1,16,2,32]{3,1,2,0:T(8,128)S(1)}, f32[1,16,2,32]{3,1,2,0:T(8,128)S(1)}, u32[]{:S(2)}, u32[]{:S(2)}) collective-permute-start(f32[1,16,2,32]{3,1,2,0:T(8,128)S(1)} %maximum_bitcast_fusion.3), channel_id=1, source_target_pairs={{4,0},{8,4},{12,8},{16,12},{20,16},{24,20},{28,24},{0,28},{5,1},{9... | collective-permute-start | bytes 12296 | tf_op jit(solution)/shard_map/ppermute | solution.py:24
  110.0 8.4 %collective-permute-start.12 = (f32[1,16,2,32]{3,1,2,0:T(8,128)S(1)}, f32[1,16,2,32]{3,1,2,0:T(8,128)S(1)}, u32[]{:S(2)}, u32[]{:S(2)}) collective-permute-start(f32[1,16,2,32]{3,1,2,0:T(8,128)S(1)} %maximum_bitcast_fusion.3), channel_id=1, source_target_pairs={{0,4},{4,8},{8,12},{12,16},{16,20},{20,24},{24,28},{28,0},{1,5},{5... | collective-permute-start | bytes 12296 | tf_op jit(solution)/shard_map/ppermute | solution.py:22
  110.6 7.7 %collective-permute-start.14 = (f32[16,2,32]{2,1,0:T(2,128)S(1)}, f32[16,2,32]{2,1,0:T(2,128)S(1)}, u32[]{:S(2)}, u32[]{:S(2)}) collective-permute-start(f32[16,2,32]{2,1,0:T(2,128)S(1)} %pad_maximum_fusion.3), channel_id=1, source_target_pairs={{0,16},{4,20},{8,24},{12,28},{16,0},{20,4},{24,8},{28,12},{1,17},{... | collective-permute-start | bytes 12296 | tf_op jit(solution)/shard_map/ppermute | solution.py:33
  114.4 9.6 %all-to-all-start.6 = ((bf16[4,2,2048]{2,1,0:T(2,128)(2,1)}), bf16[4,2,2048]{2,1,0:T(2,128)(2,1)}, u32[]{:S(2)}, u32[]{:S(2)}) async-start(bf16[4,2,2048]{2,1,0:T(2,128)(2,1)} %reshape.258), calls=%async_computation.6 | async-start | bytes 65536 | tf_op jit(solution)/shard_map/all_to_all | solution.py:117
  118.3 145.7 %all-reduce.4.cloned.1.call-start = ((), (), s32[]{:S(2)}) async-start(), calls=%async_computation.8 | async-start | bytes 3932160 | tf_op jit(solution)/shard_map/psum | solution.py:150
  120.2 7.4 %copy-start.14 = (bf16[640,64]{0,1:T(8,128)(2,1)S(1)}, bf16[640,64]{0,1:T(8,128)(2,1)}, u32[]{:S(2)}) copy-start(bf16[640,64]{0,1:T(8,128)(2,1)} %param.18) | copy-start | bytes 245764
  129.0 0.9 copy-start.6
  129.0 0.9 copy-start.20
  129.1 1.8 copy-start.1
  132.5 0.8 copy-start.18
  132.5 5.0 %copy-start.24 = (f32[640]{0:T(1024)S(1)}, f32[640]{0:T(1024)}, u32[]{:S(2)}) copy-start(f32[640]{0:T(1024)} %get-tuple-element.77) | copy-start | bytes 7684
  134.3 45.1 %all-to-all-start.7 = ((f32[2,32,256]{2,0,1:T(2,128)}), f32[2,32,256]{2,0,1:T(2,128)S(1)}, u32[]{:S(2)}, u32[]{:S(2)}) async-start(f32[2,32,256]{2,0,1:T(2,128)} %copy.182), calls=%async_computation.7 | async-start | bytes 131072 | tf_op jit(solution)/shard_map/all_to_all | solution.py:122
Sparse Core Ops, SparseCore 0:
  132.7 131.2 all-reduce.3
where the time goes:
time: 278 us; the launch traced here: 277 us
  waiting for transfers between devices  109 us (39%)
  starting transfers between devices  45.2 us (16%)
  blocking collectives  40 us (14%)
  local copies, waits for them, and re-layouts  32.6 us (12%)
  other arithmetic  17.3 us (6%)
  matrix products  17.3 us (6%)
  between operations  15 us (5%)
    psum x1, waiting for transfers between devices, body(): summed = lax.psum(totals, ('tile', 'depth'))  84 us
    psum x1, blocking collectives, body(): summed = lax.psum(totals, ('tile', 'depth'))  40 us
    all_to_all x4, starting transfers between devices, to_columns(): lax.all_to_all(segment, 'depth', split_axis=2, concat_axis=1, tiled=True)  16.1 us
    all_to_all x4, starting transfers between devices, to_segments(): lax.all_to_all(shaped, 'depth', split_axis=1, concat_axis=2, tiled=True)  15.6 us
    all_to_all x4, waiting for transfers between devices, to_segments(): lax.all_to_all(shaped, 'depth', split_axis=1, concat_axis=2, tiled=True)  13.8 us
    unnamed x64, local copies, waits for them, and re-layouts  10.7 us
    all_to_all x4, waiting for transfers between devices, to_columns(): lax.all_to_all(segment, 'depth', split_axis=2, concat_axis=1, tiled=True)  9.74 us
    ppermute x5, starting transfers between devices, with_halo(): lax.ppermute(head, axis, [((i + 1) % count, i) for i in range(count)])  6.25 us
  transfers between devices with their start and end apart: 24, of which 8 were waited for; matrix products, arithmetic and copies ran while one was open for 11% of the time, Pallas kernels for 0%

commit v1 on v0

--- a/solution.py
+++ b/solution.py
@@ -10,6 +10,13 @@
 TILE_CELLS = 1024
 diffuse_coef = 0.2
 step_size = 0.5
+
+
+def swap_blocks(block, name, split, join):
+    size = lax.axis_size(name)
+    parts = jnp.stack(jnp.split(block, size, axis=split), axis=0)
+    parts = lax.all_to_all(parts, name, split_axis=0, concat_axis=0)
+    return jnp.concatenate(parts, axis=join)
 
 
 def with_halo(cells, sides, width):
@@ -114,7 +121,7 @@
     weight_sums = neighbour_sum(weight[None, :])[0]
 
     def to_columns(segment):
-        full_cols = lax.all_to_all(segment, "depth", split_axis=2, concat_axis=1, tiled=True)
+        full_cols = swap_blocks(segment, "depth", 2, 1)
         return full_cols.reshape(FEATURES, full_cols.shape[2])
 
     def to_segments(values):

time: 278 us -> 289 us (1.040)
  other arithmetic: 17.3 us -> 25.4 us
    unnamed x64 -> x66, local copies, waits for them, and re-layouts: 10.7 us -> 1.08 us
    all_to_all x4, waiting for transfers between devices: 9.74 us -> 5.64 us  [swap_blocks(): parts = lax.all_to_all(parts, name, split_axis=0, concat_axis=0)]
    psum x1, waiting for transfers between devices: 84 us -> 87.2 us  [body(): summed = lax.psum(totals, ('tile', 'depth'))]
  transfers between devices with their start and end apart: 24 -> 24, of which waited for: 8 -> 7; matrix products, arithmetic and copies ran while one was open for 11% -> 14% of each run, Pallas kernels for 0% -> 0%
where the time goes in v1:
time: 289 us; the launch traced here: 287 us
  waiting for transfers between devices  108 us (37%)
  starting transfers between devices  46.8 us (16%)
  blocking collectives  40.2 us (14%)
  local copies, waits for them, and re-layouts  34.9 us (12%)
  other arithmetic  25.4 us (9%)
  matrix products  17.1 us (6%)
  between operations  14.8 us (5%)
    psum x1, waiting for transfers between devices, body(): summed = lax.psum(totals, ('tile', 'depth'))  87.2 us
    psum x1, blocking collectives, body(): summed = lax.psum(totals, ('tile', 'depth'))  40.2 us
    all_to_all x4, starting transfers between devices, to_segments(): lax.all_to_all(shaped, 'depth', split_axis=1, concat_axis=2, tiled=True)  17.7 us
    all_to_all x4, starting transfers between devices, swap_blocks(): parts = lax.all_to_all(parts, name, split_axis=0, concat_axis=0)  15.4 us
    all_to_all x4, waiting for transfers between devices, to_segments(): lax.all_to_all(shaped, 'depth', split_axis=1, concat_axis=2, tiled=True)  13.3 us
    ppermute x5, starting transfers between devices, with_halo(): lax.ppermute(head, axis, [((i + 1) % count, i) for i in range(count)])  6.2 us
    add x5, other arithmetic, neighbour_sum(): west_cells + east_cells + south_cells + north_cells  6.08 us
  transfers between devices with their start and end apart: 24, of which 7 were waited for; matrix products, arithmetic and copies ran while one was open for 14% of the time, Pallas kernels for 0%

profile of v1, /device:TPU:0, one launch (start us, length us, event | category | flops | bytes accessed | tf_op | source)
XLA Modules:
  0.0 286.9 jit_solution(528740277648934418)
XLA Ops:
  7.2 0.8 convert_multiply_fusion
  8.2 3.4 %collective-permute-start.4 = (f32[1,1,2,32]{3,2,1,0:T(2,128)S(1)}, f32[1,1,2,32]{3,2,1,0:T(2,128)S(1)}, u32[]{:S(2)}, u32[]{:S(2)}) collective-permute-start(f32[1,1,2,32]{3,2,1,0:T(2,128)S(1)} %maximum_bitcast_fusion.4), channel_id=1, source_target_pairs={{4,0},{8,4},{12,8},{16,12},{20,16},{24,20},{28,24},{0,28},{5,1},{9... | collective-permute-start | bytes 776 | tf_op jit(solution)/shard_map/ppermute | solution.py:31
  11.7 1.0 reshape.226
  13.0 2.7 collective-permute-start.1
  16.3 0.8 convert_element_type.60
  17.8 5.0 %all-to-all-start = ((bf16[4,2,8,256]{3,2,1,0:T(8,128)(2,1)}), bf16[4,2,8,256]{3,2,1,0:T(8,128)(2,1)S(1)}, u32[]{:S(2)}, u32[]{:S(2)}) async-start(bf16[4,2,8,256]{3,2,1,0:T(8,128)(2,1)} %pad_maximum_fusion), calls=%async_computation | async-start | bytes 65536 | tf_op jit(solution)/shard_map/all_to_all | solution.py:18
  24.4 1.5 collective-permute-start.2
  26.5 1.7 collective-permute-done.2
  30.6 1.3 multiply_convert_fusion.2
  32.9 5.1 %all-to-all-start.1 = ((f32[2,32,256]{2,0,1:T(2,128)}), f32[2,32,256]{2,0,1:T(2,128)}, u32[]{:S(2)}, u32[]{:S(2)}) async-start(f32[2,32,256]{2,0,1:T(2,128)} %copy.117), calls=%async_computation.1 | async-start | bytes 131072 | tf_op jit(solution)/shard_map/all_to_all | solution.py:129
  38.0 1.2 fusion.13
  39.3 4.5 %all-to-all-done.1 = f32[2,32,256]{2,0,1:T(2,128)} async-done(((f32[2,32,256]{2,0,1:T(2,128)}), f32[2,32,256]{2,0,1:T(2,128)}, u32[]{:S(2)}, u32[]{:S(2)}) %all-to-all-start.1) | async-done | bytes 65568 | tf_op jit(solution)/shard_map/all_to_all | solution.py:129
  43.8 0.8 copy.118
  46.0 0.8 fusion.30
  46.8 1.6 collective-permute-start.8
  49.0 3.3 %all-to-all-start.2 = ((bf16[4,2,8,256]{3,2,1,0:T(8,128)(2,1)}), bf16[4,2,8,256]{3,2,1,0:T(8,128)(2,1)S(1)}, u32[]{:S(2)}, u32[]{:S(2)}) async-start(bf16[4,2,8,256]{3,2,1,0:T(8,128)(2,1)} %pad_maximum_fusion.1), calls=%async_computation.2 | async-start | bytes 65536 | tf_op jit(solution)/shard_map/all_to_all | solution.py:18
  54.2 3.8 %all-to-all-done.2 = bf16[4,2,8,256]{3,2,1,0:T(8,128)(2,1)S(1)} async-done(((bf16[4,2,8,256]{3,2,1,0:T(8,128)(2,1)}), bf16[4,2,8,256]{3,2,1,0:T(8,128)(2,1)S(1)}, u32[]{:S(2)}, u32[]{:S(2)}) %all-to-all-start.2) | async-done | bytes 32800 | tf_op jit(solution)/shard_map/all_to_all | solution.py:18
  58.9 1.3 multiply_convert_fusion
  61.1 3.9 %all-to-all-start.3 = ((f32[2,32,256]{2,0,1:T(2,128)}), f32[2,32,256]{2,0,1:T(2,128)}, u32[]{:S(2)}, u32[]{:S(2)}) async-start(f32[2,32,256]{2,0,1:T(2,128)} %copy.122), calls=%async_computation.3 | async-start | bytes 131072 | tf_op jit(solution)/shard_map/all_to_all | solution.py:129
  65.0 1.3 fusion.15
  66.5 4.4 %all-to-all-done.3 = f32[2,32,256]{2,0,1:T(2,128)} async-done(((f32[2,32,256]{2,0,1:T(2,128)}), f32[2,32,256]{2,0,1:T(2,128)}, u32[]{:S(2)}, u32[]{:S(2)}) %all-to-all-start.3) | async-done | bytes 65568 | tf_op jit(solution)/shard_map/all_to_all | solution.py:129
  70.8 0.8 copy.123
  71.7 1.5 multiply_convert_fusion.5
  74.4 0.9 fusion.27
  76.5 3.9 %all-to-all-start.4 = ((bf16[4,2,8,256]{3,2,1,0:T(8,128)(2,1)}), bf16[4,2,8,256]{3,2,1,0:T(8,128)(2,1)}, u32[]{:S(2)}, u32[]{:S(2)}) async-start(bf16[4,2,8,256]{3,2,1,0:T(8,128)(2,1)} %pad_maximum_fusion.2), calls=%async_computation.4 | async-start | bytes 65536 | tf_op jit(solution)/shard_map/all_to_all | solution.py:18
  82.2 1.3 fusion.17
  83.5 0.8 add.296
  84.3 1.8 all-to-all-done.4
  86.1 0.8 copy.126
  86.9 0.8 fusion.47
  87.7 2.2 convert_reduce_fusion.1
  89.9 1.1 convert_reduce_fusion.3
  91.2 0.9 fusion.46
  93.3 3.9 %all-to-all-start.5 = ((f32[2,32,256]{2,0,1:T(2,128)}), f32[2,32,256]{2,0,1:T(2,128)}, u32[]{:S(2)}, u32[]{:S(2)}) async-start(f32[2,32,256]{2,0,1:T(2,128)} %copy.127), calls=%async_computation.5 | async-start | bytes 131072 | tf_op jit(solution)/shard_map/all_to_all | solution.py:129
  97.2 1.4 convert_reduce_fusion.5
  98.6 4.4 %all-to-all-done.5 = f32[2,32,256]{2,0,1:T(2,128)} async-done(((f32[2,32,256]{2,0,1:T(2,128)}), f32[2,32,256]{2,0,1:T(2,128)}, u32[]{:S(2)}, u32[]{:S(2)}) %all-to-all-start.5) | async-done | bytes 65568 | tf_op jit(solution)/shard_map/all_to_all | solution.py:129
  103.0 0.8 copy.128
  103.9 1.5 multiply_convert_fusion.4
  105.4 1.7 reshape.235
  107.1 1.0 broadcast_multiply_fusion.1
  109.5 0.9 fusion.26
  110.4 0.8 fusion.24
  111.9 1.5 collective-permute-start.14
  114.0 3.3 %all-to-all-start.6 = ((bf16[4,2,8,256]{3,2,1,0:T(8,128)(2,1)}), bf16[4,2,8,256]{3,2,1,0:T(8,128)(2,1)S(1)}, u32[]{:S(2)}, u32[]{:S(2)}) async-start(bf16[4,2,8,256]{3,2,1,0:T(8,128)(2,1)} %pad_maximum_fusion.3), calls=%async_computation.6 | async-start | bytes 65536 | tf_op jit(solution)/shard_map/all_to_all | solution.py:18
  117.5 1.4 fusion.36
  118.9 1.3 slice_bitcast_fusion.5
  120.2 1.4 slice.279
  121.6 1.4 slice.275
  123.0 1.6 copy.129
  124.6 1.3 slice_bitcast_fusion.4
  125.9 1.6 copy.130
  127.4 2.3 fusion.19
  129.7 1.7 add.304
  131.4 1.8 convolution_add_fusion.5
  133.2 2.1 convert_reduce_fusion
  135.3 1.1 convert_reduce_fusion.2
  136.4 1.7 convolution_add_fusion
  138.1 0.9 convolution_add_fusion.6
  140.1 4.8 %all-to-all-start.7 = ((f32[2,32,256]{2,0,1:T(2,128)}), f32[2,32,256]{2,0,1:T(2,128)S(1)}, u32[]{:S(2)}, u32[]{:S(2)}) async-start(f32[2,32,256]{2,0,1:T(2,128)} %copy.132), calls=%async_computation.7 | async-start | bytes 131072 | tf_op jit(solution)/shard_map/all_to_all | solution.py:129
  145.0 40.2 %all-reduce = (f32[640]{0:T(1024)S(1)}, f32[640]{0:T(1024)S(1)}, f32[64]{0:T(128)S(1)}) all-reduce(f32[640]{0:T(1024)S(1)} %add.310, f32[640]{0:T(1024)S(1)} %add.312, f32[64]{0:T(128)S(1)} %add.315), channel_id=1, replica_groups=mesh['tile'=8,'depth'=4] {'tile','depth'}, use_global_device_ids=true, to_apply=%region_3.4 | all-reduce | flops 1344 | bytes 10752 | tf_op jit(solution)/shard_map/psum | solution.py:157
  187.0 87.2 %all-reduce.4.cloned.1.call-done = (f32[64,640]{1,0:T(8,128)}, f32[640,640]{1,0:T(8,128)}, f32[640,64]{0,1:T(8,128)}) async-done(((f32[64,640]{1,0:T(8,128)}, f32[640,640]{1,0:T(8,128)}, f32[640,64]{0,1:T(8,128)}), (f32[64,640]{1,0:T(8,128)}, f32[640,640]{1,0:T(8,128)}, f32[640,64]{0,1:T(8,128)})) %all-reduce.4.cloned.1.call-update) | async-done | bytes 1966096 | tf_op jit(solution)/shard_map/psum | solution.py:157
  274.2 1.6 broadcast_multiply_fusion.6
  275.8 1.6 broadcast_multiply_fusion.5
  277.4 2.7 broadcast_multiply_fusion
  (194 shorter events, 24.6 us)
Async XLA Ops:
  7.2 23.5 %copy-start = (bf16[640,640]{1,0:T(8,128)(2,1)S(1)}, bf16[640,640]{1,0:T(8,128)(2,1)}, u32[]{:S(2)}) copy-start(bf16[640,640]{1,0:T(8,128)(2,1)} %param.16) | copy-start | bytes 2457604
  8.0 95.9 %copy-start.16 = (f32[1024]{0:T(1024)}, f32[1024]{0:T(1024)S(1)}, u32[]{:S(2)}) copy-start(f32[1024]{0:T(1024)S(1)} %get-tuple-element.85) | copy-start | bytes 12292
  8.2 18.0 %collective-permute-start.4 = (f32[1,1,2,32]{3,2,1,0:T(2,128)S(1)}, f32[1,1,2,32]{3,2,1,0:T(2,128)S(1)}, u32[]{:S(2)}, u32[]{:S(2)}) collective-permute-start(f32[1,1,2,32]{3,2,1,0:T(2,128)S(1)} %maximum_bitcast_fusion.4), channel_id=1, source_target_pairs={{4,0},{8,4},{12,8},{16,12},{20,16},{24,20},{28,24},{0,28},{5,1},{9... | collective-permute-start | bytes 776 | tf_op jit(solution)/shard_map/ppermute | solution.py:31
  11.6 12.8 %collective-permute-start.3 = (f32[1,1,2,32]{3,2,1,0:T(2,128)S(1)}, f32[1,1,2,32]{3,2,1,0:T(2,128)S(1)}, u32[]{:S(2)}, u32[]{:S(2)}) collective-permute-start(f32[1,1,2,32]{3,2,1,0:T(2,128)S(1)} %maximum_bitcast_fusion.4), channel_id=1, source_target_pairs={{0,4},{4,8},{8,12},{12,16},{16,20},{20,24},{24,28},{28,0},{1,5},{5... | collective-permute-start | bytes 776 | tf_op jit(solution)/shard_map/ppermute | solution.py:29
  12.7 11.1 %copy-start.24 = (s32[1024]{0:T(1024)S(1)}, s32[1024]{0:T(1024)}, u32[]{:S(2)}) copy-start(s32[1024]{0:T(1024)} %param.13) | copy-start | bytes 12292
  13.0 15.1 %collective-permute-start.1 = (f32[1,16,2,32]{3,1,2,0:T(8,128)S(1)}, f32[1,16,2,32]{3,1,2,0:T(8,128)S(1)}, u32[]{:S(2)}, u32[]{:S(2)}) collective-permute-start(f32[1,16,2,32]{3,1,2,0:T(8,128)S(1)} %maximum_bitcast_fusion), channel_id=1, source_target_pairs={{4,0},{8,4},{12,8},{16,12},{20,16},{24,20},{28,24},{0,28},{5,1},{9... | collective-permute-start | bytes 12296 | tf_op jit(solution)/shard_map/ppermute | solution.py:31
  15.7 12.5 %collective-permute-start = (f32[1,16,2,32]{3,1,2,0:T(8,128)S(1)}, f32[1,16,2,32]{3,1,2,0:T(8,128)S(1)}, u32[]{:S(2)}, u32[]{:S(2)}) collective-permute-start(f32[1,16,2,32]{3,1,2,0:T(8,128)S(1)} %maximum_bitcast_fusion), channel_id=1, source_target_pairs={{0,4},{4,8},{8,12},{12,16},{16,20},{20,24},{24,28},{28,0},{1,5},{5... | collective-permute-start | bytes 12296 | tf_op jit(solution)/shard_map/ppermute | solution.py:29
  15.8 10.2 %collective-permute-start.5 = (f32[1,2,32]{2,1,0:T(2,128)S(1)}, f32[1,2,32]{2,1,0:T(2,128)S(1)}, u32[]{:S(2)}, u32[]{:S(2)}) collective-permute-start(f32[1,2,32]{2,1,0:T(2,128)S(1)} %pad_maximum_fusion.8), channel_id=1, source_target_pairs={{0,16},{4,20},{8,24},{12,28},{16,0},{20,4},{24,8},{28,12},{1,17},{... | collective-permute-start | bytes 776 | tf_op jit(solution)/shard_map/ppermute | solution.py:40
  17.8 12.2 %copy-start.1 = (bf16[64,640]{1,0:T(8,128)(2,1)S(1)}, bf16[64,640]{1,0:T(8,128)(2,1)}, u32[]{:S(2)}) copy-start(bf16[64,640]{1,0:T(8,128)(2,1)} %param.14) | copy-start | bytes 245764
  17.8 12.2 %copy-start.21 = (f32[640]{0:T(1024)S(1)}, f32[640]{0:T(1024)}, u32[]{:S(2)}) copy-start(f32[640]{0:T(1024)} %param.15) | copy-start | bytes 7684
  17.8 12.2 %all-to-all-start = ((bf16[4,2,8,256]{3,2,1,0:T(8,128)(2,1)}), bf16[4,2,8,256]{3,2,1,0:T(8,128)(2,1)S(1)}, u32[]{:S(2)}, u32[]{:S(2)}) async-start(bf16[4,2,8,256]{3,2,1,0:T(8,128)(2,1)} %pad_maximum_fusion), calls=%async_computation | async-start | bytes 65536 | tf_op jit(solution)/shard_map/all_to_all | solution.py:18
  23.0 7.6 %copy-start.31 = (f32[640]{0:T(1024)S(1)}, f32[640]{0:T(1024)}, u32[]{:S(2)}) copy-start(f32[640]{0:T(1024)} %param.17) | copy-start | bytes 7684
  24.4 3.7 %collective-permute-start.2 = (f32[16,2,32]{2,1,0:T(2,128)S(1)}, f32[16,2,32]{2,1,0:T(2,128)S(1)}, u32[]{:S(2)}, u32[]{:S(2)}) collective-permute-start(f32[16,2,32]{2,1,0:T(2,128)S(1)} %pad_maximum_fusion.4), channel_id=1, source_target_pairs={{0,16},{4,20},{8,24},{12,28},{16,0},{20,4},{24,8},{28,12},{1,17},{... | collective-permute-start | bytes 12296 | tf_op jit(solution)/shard_map/ppermute | solution.py:40
  26.5 77.4 %copy-start.19 = (f32[1024]{0:T(1024)}, f32[1024]{0:T(1024)S(1)}, u32[]{:S(2)}) copy-start(f32[1024]{0:T(1024)S(1)} %add.265) | copy-start | bytes 12292
  30.0 0.6 copy-start.13
  30.6 1.4 copy-start.9
  30.6 1.4 copy-start.29
  32.0 12.7 %copy-start.7 = (f32[2,8,1024]{2,1,0:T(8,128)S(1)}, f32[2,8,1024]{2,1,0:T(8,128)}, u32[]{:S(2)}) copy-start(f32[2,8,1024]{2,1,0:T(8,128)} %param.10) | copy-start | bytes 196612
  32.9 10.9 %all-to-all-start.1 = ((f32[2,32,256]{2,0,1:T(2,128)}), f32[2,32,256]{2,0,1:T(2,128)}, u32[]{:S(2)}, u32[]{:S(2)}) async-start(f32[2,32,256]{2,0,1:T(2,128)} %copy.117), calls=%async_computation.1 | async-start | bytes 131072 | tf_op jit(solution)/shard_map/all_to_all | solution.py:129
  44.7 2.1 copy-start.6
  45.2 7.1 %collective-permute-start.7 = (f32[1,16,2,32]{3,1,2,0:T(8,128)S(1)}, f32[1,16,2,32]{3,1,2,0:T(8,128)S(1)}, u32[]{:S(2)}, u32[]{:S(2)}) collective-permute-start(f32[1,16,2,32]{3,1,2,0:T(8,128)S(1)} %maximum_bitcast_fusion.1), channel_id=1, source_target_pairs={{4,0},{8,4},{12,8},{16,12},{20,16},{24,20},{28,24},{0,28},{5,1},{9... | collective-permute-start | bytes 12296 | tf_op jit(solution)/shard_map/ppermute | solution.py:31
  45.3 7.1 %collective-permute-start.6 = (f32[1,16,2,32]{3,1,2,0:T(8,128)S(1)}, f32[1,16,2,32]{3,1,2,0:T(8,128)S(1)}, u32[]{:S(2)}, u32[]{:S(2)}) collective-permute-start(f32[1,16,2,32]{3,1,2,0:T(8,128)S(1)} %maximum_bitcast_fusion.1), channel_id=1, source_target_pairs={{0,4},{4,8},{8,12},{12,16},{16,20},{20,24},{24,28},{28,0},{1,5},{5... | collective-permute-start | bytes 12296 | tf_op jit(solution)/shard_map/ppermute | solution.py:29
  45.9 12.9 %copy-start.32 = (f32[640]{0:T(1024)S(1)}, f32[640]{0:T(1024)}, u32[]{:S(2)}) copy-start(f32[640]{0:T(1024)} %param.17) | copy-start | bytes 7684
  46.8 5.5 %collective-permute-start.8 = (f32[16,2,32]{2,1,0:T(2,128)S(1)}, f32[16,2,32]{2,1,0:T(2,128)S(1)}, u32[]{:S(2)}, u32[]{:S(2)}) collective-permute-start(f32[16,2,32]{2,1,0:T(2,128)S(1)} %pad_maximum_fusion.5), channel_id=1, source_target_pairs={{0,16},{4,20},{8,24},{12,28},{16,0},{20,4},{24,8},{28,12},{1,17},{... | collective-permute-start | bytes 12296 | tf_op jit(solution)/shard_map/ppermute | solution.py:40
  49.0 8.9 %all-to-all-start.2 = ((bf16[4,2,8,256]{3,2,1,0:T(8,128)(2,1)}), bf16[4,2,8,256]{3,2,1,0:T(8,128)(2,1)S(1)}, u32[]{:S(2)}, u32[]{:S(2)}) async-start(bf16[4,2,8,256]{3,2,1,0:T(8,128)(2,1)} %pad_maximum_fusion.1), calls=%async_computation.2 | async-start | bytes 65536 | tf_op jit(solution)/shard_map/all_to_all | solution.py:18
  57.9 0.6 copy-start.11
  58.8 1.4 copy-start.2
  58.8 1.4 copy-start.10
  58.9 1.4 copy-start.30
  60.2 11.5 %copy-start.22 = (f32[1024]{0:T(1024)S(1)}, f32[1024]{0:T(1024)}, u32[]{:S(2)}) copy-start(f32[1024]{0:T(1024)} %convert_element_type.59) | copy-start | bytes 12292
  61.1 9.7 %all-to-all-start.3 = ((f32[2,32,256]{2,0,1:T(2,128)}), f32[2,32,256]{2,0,1:T(2,128)}, u32[]{:S(2)}, u32[]{:S(2)}) async-start(f32[2,32,256]{2,0,1:T(2,128)} %copy.122), calls=%async_computation.3 | async-start | bytes 131072 | tf_op jit(solution)/shard_map/all_to_all | solution.py:129
  73.2 2.1 copy-start.5
  73.7 8.3 %collective-permute-start.10 = (f32[1,16,2,32]{3,1,2,0:T(8,128)S(1)}, f32[1,16,2,32]{3,1,2,0:T(8,128)S(1)}, u32[]{:S(2)}, u32[]{:S(2)}) collective-permute-start(f32[1,16,2,32]{3,1,2,0:T(8,128)S(1)} %maximum_bitcast_fusion.2), channel_id=1, source_target_pairs={{4,0},{8,4},{12,8},{16,12},{20,16},{24,20},{28,24},{0,28},{5,1},{9... | collective-permute-start | bytes 12296 | tf_op jit(solution)/shard_map/ppermute | solution.py:31
  73.8 6.6 %collective-permute-start.9 = (f32[1,16,2,32]{3,1,2,0:T(8,128)S(1)}, f32[1,16,2,32]{3,1,2,0:T(8,128)S(1)}, u32[]{:S(2)}, u32[]{:S(2)}) collective-permute-start(f32[1,16,2,32]{3,1,2,0:T(8,128)S(1)} %maximum_bitcast_fusion.2), channel_id=1, source_target_pairs={{0,4},{4,8},{8,12},{12,16},{16,20},{20,24},{24,28},{28,0},{1,5},{5... | collective-permute-start | bytes 12296 | tf_op jit(solution)/shard_map/ppermute | solution.py:29
  75.3 5.1 %collective-permute-start.11 = (f32[16,2,32]{2,1,0:T(2,128)S(1)}, f32[16,2,32]{2,1,0:T(2,128)S(1)}, u32[]{:S(2)}, u32[]{:S(2)}) collective-permute-start(f32[16,2,32]{2,1,0:T(2,128)S(1)} %pad_maximum_fusion.6), channel_id=1, source_target_pairs={{0,16},{4,20},{8,24},{12,28},{16,0},{20,4},{24,8},{28,12},{1,17},{... | collective-permute-start | bytes 12296 | tf_op jit(solution)/shard_map/ppermute | solution.py:40
  76.5 9.6 %all-to-all-start.4 = ((bf16[4,2,8,256]{3,2,1,0:T(8,128)(2,1)}), bf16[4,2,8,256]{3,2,1,0:T(8,128)(2,1)}, u32[]{:S(2)}, u32[]{:S(2)}) async-start(bf16[4,2,8,256]{3,2,1,0:T(8,128)(2,1)} %pad_maximum_fusion.2), calls=%async_computation.4 | async-start | bytes 65536 | tf_op jit(solution)/shard_map/all_to_all | solution.py:18
  87.7 2.2 copy-start.3
  89.9 1.3 copy-start.12
  93.3 9.7 %all-to-all-start.5 = ((f32[2,32,256]{2,0,1:T(2,128)}), f32[2,32,256]{2,0,1:T(2,128)}, u32[]{:S(2)}, u32[]{:S(2)}) async-start(f32[2,32,256]{2,0,1:T(2,128)} %copy.127), calls=%async_computation.5 | async-start | bytes 131072 | tf_op jit(solution)/shard_map/all_to_all | solution.py:129
  107.1 4.2 %copy-start.18 = (bf16[2,8,1024]{2,1,0:T(8,128)(2,1)S(1)}, bf16[2,8,1024]{2,1,0:T(8,128)(2,1)}, u32[]{:S(2)}) copy-start(bf16[2,8,1024]{2,1,0:T(8,128)(2,1)} %get-tuple-element.24) | copy-start | bytes 98308
  109.0 15.6 %collective-permute-start.13 = (f32[1,16,2,32]{3,1,2,0:T(8,128)}, f32[1,16,2,32]{3,1,2,0:T(8,128)}, u32[]{:S(2)}, u32[]{:S(2)}) collective-permute-start(f32[1,16,2,32]{3,1,2,0:T(8,128)} %maximum_bitcast_fusion.3), channel_id=1, source_target_pairs={{4,0},{8,4},{12,8},{16,12},{20,16},{24,20},{28,24},{0,28},{5,1},{9... | collective-permute-start | bytes 12296 | tf_op jit(solution)/shard_map/ppermute | solution.py:31
  109.0 9.9 %collective-permute-start.12 = (f32[1,16,2,32]{3,1,2,0:T(8,128)}, f32[1,16,2,32]{3,1,2,0:T(8,128)}, u32[]{:S(2)}, u32[]{:S(2)}) collective-permute-start(f32[1,16,2,32]{3,1,2,0:T(8,128)} %maximum_bitcast_fusion.3), channel_id=1, source_target_pairs={{0,4},{4,8},{8,12},{12,16},{16,20},{20,24},{24,28},{28,0},{1,5},{5... | collective-permute-start | bytes 12296 | tf_op jit(solution)/shard_map/ppermute | solution.py:29
  111.9 5.6 %collective-permute-start.14 = (f32[16,2,32]{2,1,0:T(2,128)}, f32[16,2,32]{2,1,0:T(2,128)}, u32[]{:S(2)}, u32[]{:S(2)}) collective-permute-start(f32[16,2,32]{2,1,0:T(2,128)} %pad_maximum_fusion.7), channel_id=1, source_target_pairs={{0,16},{4,20},{8,24},{12,28},{16,0},{20,4},{24,8},{28,12},{1,17},{... | collective-permute-start | bytes 12296 | tf_op jit(solution)/shard_map/ppermute | solution.py:40
  114.0 17.4 %all-to-all-start.6 = ((bf16[4,2,8,256]{3,2,1,0:T(8,128)(2,1)}), bf16[4,2,8,256]{3,2,1,0:T(8,128)(2,1)S(1)}, u32[]{:S(2)}, u32[]{:S(2)}) async-start(bf16[4,2,8,256]{3,2,1,0:T(8,128)(2,1)} %pad_maximum_fusion.3), calls=%async_computation.6 | async-start | bytes 65536 | tf_op jit(solution)/shard_map/all_to_all | solution.py:18
  117.2 156.9 %all-reduce.4.cloned.1.call-start = ((), (), s32[]{:S(2)}) async-start(), calls=%async_computation.8 | async-start | bytes 3932160 | tf_op jit(solution)/shard_map/psum | solution.py:157
  136.4 1.7 copy-start.4
  136.4 1.7 copy-start.14
  138.1 1.0 copy-start.23
  138.1 6.9 %copy-start.25 = (f32[640]{0:T(1024)S(1)}, f32[640]{0:T(1024)}, u32[]{:S(2)}) copy-start(f32[640]{0:T(1024)} %get-tuple-element.97) | copy-start | bytes 7684
  138.1 6.9 %copy-start.27 = (f32[640]{0:T(1024)S(1)}, f32[640]{0:T(1024)}, u32[]{:S(2)}) copy-start(f32[640]{0:T(1024)} %get-tuple-element.99) | copy-start | bytes 7684
  138.1 6.9 %copy-start.26 = (f32[640]{0:T(1024)S(1)}, f32[640]{0:T(1024)}, u32[]{:S(2)}) copy-start(f32[640]{0:T(1024)} %get-tuple-element.93) | copy-start | bytes 7684
  138.1 6.9 %copy-start.28 = (f32[640]{0:T(1024)S(1)}, f32[640]{0:T(1024)}, u32[]{:S(2)}) copy-start(f32[640]{0:T(1024)} %get-tuple-element.95) | copy-start | bytes 7684
  139.0 47.3 %copy-start.8 = (f32[2,8,1024]{2,1,0:T(8,128)S(1)}, f32[2,8,1024]{2,1,0:T(8,128)}, u32[]{:S(2)}) copy-start(f32[2,8,1024]{2,1,0:T(8,128)} %get-tuple-element.25) | copy-start | bytes 196612
  139.0 47.3 %copy-start.15 = (f32[2,8,1024]{2,1,0:T(8,128)S(1)}, f32[2,8,1024]{2,1,0:T(8,128)}, u32[]{:S(2)}) copy-start(f32[2,8,1024]{2,1,0:T(8,128)} %add.304) | copy-start | bytes 196612
  139.0 47.3 %copy-start.17 = (f32[1024]{0:T(1024)S(1)}, f32[1024]{0:T(1024)}, u32[]{:S(2)}) copy-start(f32[1024]{0:T(1024)} %copy-done.16) | copy-start | bytes 12292
  139.0 47.3 %copy-start.20 = (f32[1024]{0:T(1024)S(1)}, f32[1024]{0:T(1024)}, u32[]{:S(2)}) copy-start(f32[1024]{0:T(1024)} %copy-done.19) | copy-start | bytes 12292
  140.1 46.2 %all-to-all-start.7 = ((f32[2,32,256]{2,0,1:T(2,128)}), f32[2,32,256]{2,0,1:T(2,128)S(1)}, u32[]{:S(2)}, u32[]{:S(2)}) async-start(f32[2,32,256]{2,0,1:T(2,128)} %copy.132), calls=%async_computation.7 | async-start | bytes 131072 | tf_op jit(solution)/shard_map/all_to_all | solution.py:129
Sparse Core Ops, SparseCore 0:
  139.2 134.9 all-reduce.3
